TPU v7x, 32 devices: a whole 2x2x4 slice. The times are simulated.
32 devices in a mesh: heads: 2 (over y), ctx: 16 (over z, x, core).
Axes of the slice: x: 2, y: 2, z: 4, core: 2. Of those that a mesh axis runs over, the one named last changes fastest.
Arguments:
- queries: bfloat16 [8, 4096, 128], P('heads', 'ctx'), may hold values from -6 to 6
- key_rows: bfloat16 [8, 4096, 128], P('heads', 'ctx'), may hold values from -6 to 6
- value_rows: bfloat16 [8, 4096, 128], P('heads', 'ctx'), may hold values from -6 to 6
- level_weights: float32 [8, 13, 4096], P('heads', None, 'ctx'), may hold values from 0.1 to 3
- norm_gain: float32 [8, 128], P('heads'), may hold values from 0.1 to 1.9
- grad_normed: bfloat16 [8, 4096, 128], P('heads', 'ctx'), may hold values from -6 to 6
Outputs:
- normed: bfloat16 [8, 4096, 128], P('heads', 'ctx')
- grad_queries: bfloat16 [8, 4096, 128], P('heads', 'ctx')
- grad_keys: bfloat16 [8, 4096, 128], P('heads', 'ctx')
- grad_values: bfloat16 [8, 4096, 128], P('heads', 'ctx')
- grad_level_weights: float32 [8, 13, 4096], P('heads', None, 'ctx')
All inputs are finite; a program needn't handle non-finite values.
Results may differ from a plain program's by a relative error of at most 0.006.
Values sent between devices are 32-bit elements; how exact they have to be, the bound alone decides.
A program may use at most 64 MiB of HBM per device.

v0:
```python
import math
import jax
import jax.numpy as jnp
from jax import lax
from jax.sharding import PartitionSpec as P

EPS = 1e-06
HIGH = lax.Precision.HIGHEST


def from_partner(value, axis, bit):
    mask = 2**bit
    pairs = [(source, source ^ mask) for source in range(lax.axis_size(axis))]
    return lax.ppermute(value, axis, pairs)


def level_scale(number, head_dim):
    return 2.0 ** (-max(number - 1, 0) / 2.0) / math.sqrt(head_dim)


def level_matrix(count):
    position = jnp.arange(count, dtype=jnp.int32)
    differ = jnp.bitwise_xor(position[:, None], position[None, :])
    bucket = jnp.zeros((count, count), jnp.int32)
    for exponent in range(count.bit_length() - 1):
        bucket = bucket + (differ >= 2**exponent).astype(jnp.int32)
    causal = position[None, :] <= position[:, None]
    return (bucket, causal)


def near_weights(factors, bucket, causal, head_dim):
    weights = jnp.zeros(factors[0].shape + (bucket.shape[1],), jnp.float32)
    for number in range(len(factors)):
        scaled = factors[number] * level_scale(number, head_dim)
        weights = weights + jnp.where(
            (bucket == number) & causal, scaled[..., None], jnp.float32(0.0)
        )
    return weights


def pair_level(matrix, step_bit):
    return from_partner(matrix, "ctx", step_bit)


def shards(queries, key_rows, value_rows, level_weights, norm_gain, grad_normed):
    heads_here, tokens_here, head_dim = queries.shape
    local_levels = tokens_here.bit_length()
    far_levels = lax.axis_size("ctx").bit_length() - 1
    block_index = lax.axis_index("ctx")
    width = heads_here * lax.axis_size("heads") * head_dim
    key_value = jnp.einsum("hsd,hse->hde", key_rows, value_rows, preferred_element_type=jnp.float32)
    group_sum = key_value
    far_list = []
    for step_bit in range(far_levels):
        partner = from_partner(group_sum, "ctx", step_bit)
        bit_set = block_index >> step_bit & 1
        far_list.append(jnp.where(bit_set == 1, partner, jnp.float32(0.0)))
        group_sum = group_sum + partner
    states = jnp.stack(far_list, 0)
    bucket, causal = level_matrix(tokens_here)
    weights = near_weights(
        [level_weights[:, number, :] for number in range(local_levels)], bucket, causal, head_dim
    )
    scores = jnp.einsum("htd,hsd->hts", queries, key_rows, preferred_element_type=jnp.float32)
    weighted = (weights * scores).astype(jnp.bfloat16)
    near_out = jnp.einsum("hts,hse->hte", weighted, value_rows, preferred_element_type=jnp.float32)
    far_scale = jnp.stack(
        [
            level_weights[:, local_levels + depth, :] * level_scale(local_levels + depth, head_dim)
            for depth in range(far_levels)
        ],
        0,
    )
    query_wide = queries.astype(jnp.float32)
    far_terms = jnp.einsum("htd,mhde->mhte", query_wide, states, precision=HIGH)
    attended = near_out + jnp.sum(far_scale[..., None] * far_terms, 0)
    totals = lax.psum(jnp.sum(attended * attended, axis=(0, 2)), "heads")
    inv_rms = lax.rsqrt(totals / width + EPS)
    normed = (attended * inv_rms[None, :, None] * norm_gain[:, None, :]).astype(jnp.bfloat16)
    scaled = norm_gain[:, None, :] * grad_normed.astype(jnp.float32)
    inner_sum = lax.psum(jnp.sum(scaled * attended, axis=(0, 2)), "heads")
    grad_out = (
        inv_rms[None, :, None] * scaled - attended * (inv_rms**3 * inner_sum / width)[None, :, None]
    ).astype(jnp.bfloat16)
    grad_wide = grad_out.astype(jnp.float32)
    grad_mix = jnp.einsum("hte,hse->hts", grad_out, value_rows, preferred_element_type=jnp.float32)
    product = grad_mix * scores
    near_grads = [
        level_scale(number, head_dim)
        * jnp.sum(jnp.where((bucket == number) & causal, product, jnp.float32(0.0)), axis=2)
        for number in range(local_levels)
    ]
    far_grads = [
        level_scale(local_levels + depth, head_dim) * jnp.sum(grad_wide * far_terms[depth], axis=2)
        for depth in range(far_levels)
    ]
    grad_scores = (weights * grad_mix).astype(jnp.bfloat16)
    grad_q = jnp.einsum("hts,hsd->htd", grad_scores, key_rows, preferred_element_type=jnp.float32)
    grad_q = grad_q + jnp.sum(
        far_scale[..., None] * jnp.einsum("hte,mhde->mhtd", grad_wide, states, precision=HIGH), 0
    )
    scaled_queries = (far_scale[..., None] * queries[None]).astype(jnp.bfloat16)
    grad_states = jnp.einsum(
        "mhtd,hte->mhde", scaled_queries, grad_out, preferred_element_type=jnp.float32
    )
    grad_kv = jnp.zeros((heads_here, head_dim, head_dim), jnp.float32)
    for depth in range(far_levels):
        level_total = grad_states[depth]
        for step_bit in range(depth + 1):
            partner = pair_level(level_total, step_bit)
            if step_bit < depth:
                level_total = level_total + partner
            else:
                bit_set = block_index >> step_bit & 1
                grad_kv = grad_kv + jnp.where(bit_set == 0, partner, jnp.float32(0.0))
    grad_kv = grad_kv.astype(jnp.bfloat16)
    grad_k = jnp.einsum("hts,htd->hsd", grad_scores, queries, preferred_element_type=jnp.float32)
    grad_k = grad_k + jnp.einsum(
        "hse,hde->hsd", value_rows, grad_kv, preferred_element_type=jnp.float32
    )
    grad_v = jnp.einsum("hts,hte->hse", weighted, grad_out, preferred_element_type=jnp.float32)
    grad_v = grad_v + jnp.einsum(
        "hsd,hde->hse", key_rows, grad_kv, preferred_element_type=jnp.float32
    )
    grad_rates = jnp.stack(near_grads + far_grads, axis=1)
    return (
        normed,
        grad_q.astype(jnp.bfloat16),
        grad_k.astype(jnp.bfloat16),
        grad_v.astype(jnp.bfloat16),
        grad_rates,
    )


def solution(mesh):
    in_specs = (
        P("heads", "ctx", None),
        P("heads", "ctx", None),
        P("heads", "ctx", None),
        P("heads", None, "ctx"),
        P("heads", None),
        P("heads", "ctx", None),
    )
    out_specs = (
        P("heads", "ctx", None),
        P("heads", "ctx", None),
        P("heads", "ctx", None),
        P("heads", "ctx", None),
        P("heads", None, "ctx"),
    )
    return jax.shard_map(shards, mesh=mesh, in_specs=in_specs, out_specs=out_specs, check_vma=False)
```

profile of v0, /device:TPU:0, one launch (start us, length us, event | category | flops | bytes accessed | tf_op | source)
XLA Modules:
  0.0 86.8 jit_solution(17006751572486609093)
XLA Ops:
  0.7 0.9 %copy-done = bf16[4,256,128]{2,1,0:T(8,128)(2,1)S(1)} copy-done((bf16[4,256,128]{2,1,0:T(8,128)(2,1)S(1)}, bf16[4,256,128]{2,1,0:T(8,128)(2,1)}, u32[]{:S(2)}) %copy-start) | copy-done | bytes 262168
  1.6 1.2 %fusion.39 = f32[4,128,128]{2,1,0:T(8,128)S(1)} fusion(bf16[4,256,128]{2,1,0:T(8,128)(2,1)} %param.7, bf16[4,256,128]{2,1,0:T(8,128)(2,1)S(1)} %copy-done), kind=kOutput, calls=%fused_computation.115 | convolution fusion | flops 33554432 | bytes 786432 | tf_op jit(solution)/shard_map/hsd,hse->hde/dot_general | solution.py:51
  2.8 0.6 collective-permute-start
  3.5 0.2 fusion.22
  3.7 0.8 collective-permute-done
  4.6 2.9 %collective-permute-start.1 = (f32[4,128,128]{2,1,0:T(8,128)S(1)}, f32[4,128,128]{2,1,0:T(8,128)S(1)}, u32[]{:S(2)}, u32[]{:S(2)}) collective-permute-start(f32[4,128,128]{2,1,0:T(8,128)S(1)} %get-tuple-element.42), channel_id=1, source_target_pairs={{0,2},{1,3},{2,0},{3,1},{4,6},{5,7},{6,4},{7,5},{8,10},{9,11},{10,... | collective-permute-start | bytes 786440 | tf_op jit(solution)/shard_map/ppermute | solution.py:14
  7.8 6.3 %collective-permute-done.1 = f32[4,128,128]{2,1,0:T(8,128)S(1)} collective-permute-done((f32[4,128,128]{2,1,0:T(8,128)S(1)}, f32[4,128,128]{2,1,0:T(8,128)S(1)}, u32[]{:S(2)}, u32[]{:S(2)}) %collective-permute-start.1) | collective-permute-done | bytes 262176 | tf_op jit(solution)/shard_map/ppermute | solution.py:14
  14.1 0.7 select_bitcast_fusion.2
  14.9 1.8 %collective-permute-start.2 = (f32[4,128,128]{2,1,0:T(8,128)S(1)}, f32[4,128,128]{2,1,0:T(8,128)S(1)}, u32[]{:S(2)}, u32[]{:S(2)}) collective-permute-start(f32[4,128,128]{2,1,0:T(8,128)S(1)} %get-tuple-element.44), channel_id=1, source_target_pairs={{0,4},{1,5},{2,6},{3,7},{4,0},{5,1},{6,2},{7,3},{8,12},{9,13},{10,... | collective-permute-start | bytes 786440 | tf_op jit(solution)/shard_map/ppermute | solution.py:14
  16.9 0.9 %copy.42 = f32[4,256,128]{1,2,0:T(8,128)} copy(bf16[4,256,128]{2,1,0:T(8,128)(2,1)S(1)} %copy-done.2) | data formatting | bytes 786432 | tf_op jit(solution)/shard_map/convert_element_type | solution.py:102
  18.2 4.5 %collective-permute-done.2 = f32[4,128,128]{2,1,0:T(8,128)S(1)} collective-permute-done((f32[4,128,128]{2,1,0:T(8,128)S(1)}, f32[4,128,128]{2,1,0:T(8,128)S(1)}, u32[]{:S(2)}, u32[]{:S(2)}) %collective-permute-start.2) | collective-permute-done | bytes 262176 | tf_op jit(solution)/shard_map/ppermute | solution.py:14
  22.7 2.6 %collective-permute-start.3 = (f32[4,128,128]{2,1,0:T(8,128)S(1)}, f32[4,128,128]{2,1,0:T(8,128)S(1)}, u32[]{:S(2)}, u32[]{:S(2)}) collective-permute-start(f32[4,128,128]{2,1,0:T(8,128)S(1)} %get-tuple-element.46), channel_id=1, source_target_pairs={{0,8},{1,9},{2,10},{3,11},{4,12},{5,13},{6,14},{7,15},{8,0},{9,1},... | collective-permute-start | bytes 786440 | tf_op jit(solution)/shard_map/ppermute | solution.py:14
  25.3 2.0 %multiply_convert_fusion.3 = (bf16[4,256,256]{1,2,0:T(8,128)(2,1)S(1)}, f32[4,256,256]{1,2,0:T(8,128)}) fusion(f32[4,256]{1,0:T(4,128)S(1)} %get-tuple-element.50, pred[256,256]{0,1:T(8,128)(4,1)S(1)} %get-tuple-element.69, f32[4,256]{1,0:T(4,128)S(1)} %get-tuple-element.51, pred[256,256]{0,1:T(8,128)(4,1)S(1)} %get-tuple-element.70, ...), kind=kOutput, calls=%fused_computation.28 | convolution fusion | flops 72089600 | bytes 2723840 | tf_op jit(solution)/shard_map/htd,hsd->hts/dot_general | solution.py:64
  27.5 8.7 %collective-permute-done.3 = f32[4,128,128]{2,1,0:T(8,128)S(1)} collective-permute-done((f32[4,128,128]{2,1,0:T(8,128)S(1)}, f32[4,128,128]{2,1,0:T(8,128)S(1)}, u32[]{:S(2)}, u32[]{:S(2)}) %collective-permute-start.3) | collective-permute-done | bytes 262176 | tf_op jit(solution)/shard_map/ppermute | solution.py:14
  36.3 1.1 %multiply_reduce_fusion = (f32[4,256,128]{1,2,0:T(8,128)S(1)}, f32[4,4,256,128]{2,3,1,0:T(8,128)S(1)}) fusion(f32[4,4,256]{2,1,0:T(4,128)S(1)} %pad_maximum_fusion.3, bf16[4,256,128]{2,1,0:T(8,128)(2,1)S(1)} %copy-done.2, f32[1,4,128,128]{3,2,1,0:T(8,128)S(1)} %select_bitcast_fusion, f32[1,4,128,128]{3,2,1,0:T(8,128)S(1)} %get-tuple-element.45, ...), kind=kOutput, calls=%fused_computation.3 | convolution fusion | flops 807010304 | bytes 3948544 | tf_op jit(solution)/shard_map/htd,mhde->mhte/dot_general | solution.py:75
  37.4 1.1 %multiply_reduce_fusion.1 = (f32[256]{0:T(256)S(1)}, f32[256]{0:T(256)S(1)}, f32[4,256,128]{1,2,0:T(8,128)}) fusion(bf16[4,256,128]{1,2,0:T(8,128)(2,1)S(1)} %copy.35, f32[4,128]{1,0:T(4,128)S(1)} %copy-done.32, f32[4,256,128]{1,2,0:T(8,128)S(1)} %get-tuple-element.62, bf16[4,256,256]{1,2,0:T(8,128)(2,1)S(1)} %get-tuple-element.64, ...), kind=kOutput, calls=%fused_computation.43 | convolution fusion | flops 68025856 | bytes 2101248 | tf_op jit(solution)/shard_map/hts,hse->hte/dot_general | solution.py:66
  38.6 4.9 %all-reduce = (f32[256]{0:T(256)S(1)}, f32[256]{0:T(256)S(1)}) all-reduce(f32[256]{0:T(256)S(1)} %get-tuple-element.29, f32[256]{0:T(256)S(1)} %get-tuple-element.28), channel_id=1, replica_groups=mesh['heads'=2,'ctx'=16] {'heads'}, use_global_device_ids=true, to_apply=%region_2.3 | all-reduce | flops 512 | bytes 4096 | tf_op jit(solution)/shard_map/psum | solution.py:77
  43.5 1.4 %fusion.11 = (f32[4,256]{1,0:T(4,128)S(1)}, f32[4,256]{1,0:T(4,128)S(1)}, f32[4,256]{1,0:T(4,128)S(1)}, f32[4,256]{1,0:T(4,128)S(1)}, bf16[4,256,128]{1,2,0:T(8,128)(2,1)S(1)}, /*index=5*/bf16[4,256,128]{1,2,0:T(8,128)(2,1)S(1)}) fusion(f32[4,4,256,128]{2,3,1,0:T(8,128)S(1)} %get-tuple-element.63, f32[4,256,128]{1,2,0:T(8,128)} %get-tuple-element.66, ...), kind=kLoop, calls=%fused_computation.37 | loop fusion | flops 2355200 | bytes 3428352 | tf_op jit(solution)/shard_map/reduce_sum | solution.py:94
  45.0 2.3 %multiply_convert_fusion.2 = (bf16[4,256,256]{1,2,0:T(8,128)(2,1)S(1)}, f32[4,256,256]{1,2,0:T(8,128)S(1)}) fusion(f32[4,256]{1,0:T(4,128)} %copy-done.34, pred[256,256]{0,1:T(8,128)(4,1)S(1)} %get-tuple-element.69, f32[4,256]{1,0:T(4,128)} %copy-done.35, pred[256,256]{0,1:T(8,128)(4,1)S(1)} %get-tuple-element.70, f32[4,256]{1,0:T(4,128)} %copy-done.36, ...), kind=kOutput, calls=%fused_computation.26 | convolution fusion | flops 72089600 | bytes 2723840 | tf_op jit(solution)/shard_map/hte,hse->hts/dot_general | solution.py:86
  47.4 0.9 %select_reduce_fusion = (f32[4,256]{1,0:T(4,128)S(1)}, f32[4,256]{1,0:T(4,128)S(1)}, f32[4,256]{1,0:T(4,128)S(1)}, f32[4,256]{1,0:T(4,128)S(1)}, f32[4,256]{1,0:...) fusion(pred[256,256]{0,1:T(8,128)(4,1)S(1)} %get-tuple-element.69, ...), kind=kLoop, calls=%fused_computation.16 | loop fusion | flops 4971520 | bytes 2723840 | tf_op jit(solution)/shard_map/reduce_sum | solution.py:90
  48.3 0.4 convolution_bitcast_fusion.1
  48.8 0.8 slice_bitcast_fusion.7
  49.6 0.5 collective-permute-start.5
  50.1 0.5 collective-permute-start.4
  50.7 0.4 collective-permute-done.10
  51.1 0.4 collective-permute-done.5
  51.5 0.4 collective-permute-done.7
  51.8 0.8 fusion.36
  52.6 1.2 %collective-permute-start.11 = (f32[4,128,128]{2,1,0:T(8,128)S(1)}, f32[4,128,128]{2,1,0:T(8,128)S(1)}, u32[]{:S(2)}, u32[]{:S(2)}) collective-permute-start(f32[4,128,128]{2,1,0:T(8,128)S(1)} %get-tuple-element.38), channel_id=1, source_target_pairs={{0,2},{1,3},{2,0},{3,1},{4,6},{5,7},{6,4},{7,5},{8,10},{9,11},{10,... | collective-permute-start | bytes 786440 | tf_op jit(solution)/shard_map/ppermute | solution.py:14
  53.8 0.3 fusion.41
  54.1 0.9 %collective-permute-start.8 = (f32[4,128,128]{2,1,0:T(8,128)S(1)}, f32[4,128,128]{2,1,0:T(8,128)}, u32[]{:S(2)}, u32[]{:S(2)}) collective-permute-start(f32[4,128,128]{2,1,0:T(8,128)S(1)} %get-tuple-element.39), channel_id=1, source_target_pairs={{0,2},{1,3},{2,0},{3,1},{4,6},{5,7},{6,4},{7,5},{8,10},{9,11},{10,... | collective-permute-start | bytes 786440 | tf_op jit(solution)/shard_map/ppermute | solution.py:14
  55.0 6.8 %collective-permute-done.11 = f32[4,128,128]{2,1,0:T(8,128)S(1)} collective-permute-done((f32[4,128,128]{2,1,0:T(8,128)S(1)}, f32[4,128,128]{2,1,0:T(8,128)S(1)}, u32[]{:S(2)}, u32[]{:S(2)}) %collective-permute-start.11) | collective-permute-done | bytes 262176 | tf_op jit(solution)/shard_map/ppermute | solution.py:14
  61.8 0.4 collective-permute-start.12
  62.3 1.8 %fusion = f32[4,256,128]{1,2,0:T(8,128)} fusion(f32[4,4,256]{2,1,0:T(4,128)S(1)} %pad_maximum_fusion.3, f32[1,4,128,128]{3,2,1,0:T(8,128)S(1)} %copy-done.8, f32[1,4,128,128]{3,2,1,0:T(8,128)S(1)} %copy-done.14, f32[1,4,128,128]{3,2,1,0:T(8,128)S(1)} %copy-done.12, f32[1,4,128,128]{3,2,1,0:T(8,128)S(1)} %copy-done.10, ...), kind=kOutput, calls=%fused_computation.1 | convolution fusion | flops 807010304 | bytes 1851392 | tf_op jit(solution)/shard_map/hte,mhde->mhtd/dot_general | solution.py:100
  64.1 1.3 %copy.41 = f32[4,256,128]{2,1,0:T(8,128)S(1)} copy(f32[4,256,128]{1,2,0:T(8,128)} %fusion) | data formatting | bytes 1048576 | tf_op jit(solution)/shard_map/reduce_sum | solution.py:99
  65.4 0.8 copy.49
  66.3 0.3 fusion.40
  66.6 1.6 %collective-permute-start.6 = (f32[4,128,128]{2,1,0:T(8,128)S(1)}, f32[4,128,128]{2,1,0:T(8,128)S(1)}, u32[]{:S(2)}, u32[]{:S(2)}) collective-permute-start(f32[4,128,128]{2,1,0:T(8,128)S(1)} %copy-done.15), channel_id=1, source_target_pairs={{0,2},{1,3},{2,0},{3,1},{4,6},{5,7},{6,4},{7,5},{8,10},{9,11},{10,... | collective-permute-start | bytes 786440 | tf_op jit(solution)/shard_map/ppermute | solution.py:14
  68.1 1.0 %add.366 = f32[4,128,128]{2,1,0:T(8,128)S(1)} add(f32[4,128,128]{2,1,0:T(8,128)S(1)} %get-tuple-element.39, f32[4,128,128]{2,1,0:T(8,128)} %collective-permute-done.8) | non-fusion elementwise | flops 65536 | bytes 786432 | tf_op jit(solution)/shard_map/add | solution.py:112
  69.1 1.4 %collective-permute-start.9 = (f32[4,128,128]{2,1,0:T(8,128)S(1)}, f32[4,128,128]{2,1,0:T(8,128)S(1)}, u32[]{:S(2)}, u32[]{:S(2)}) collective-permute-start(f32[4,128,128]{2,1,0:T(8,128)S(1)} %add.366), channel_id=1, source_target_pairs={{0,4},{1,5},{2,6},{3,7},{4,0},{5,1},{6,2},{7,3},{8,12},{9,13},{10,... | collective-permute-start | bytes 786440 | tf_op jit(solution)/shard_map/ppermute | solution.py:14
  70.5 1.0 %add.370 = f32[4,128,128]{2,1,0:T(8,128)S(1)} add(f32[4,128,128]{2,1,0:T(8,128)S(1)} %add.369, f32[4,128,128]{2,1,0:T(8,128)} %collective-permute-done.12) | non-fusion elementwise | flops 65536 | bytes 786432 | tf_op jit(solution)/shard_map/add | solution.py:112
  71.5 2.1 %collective-permute-start.13 = (f32[4,128,128]{2,1,0:T(8,128)S(1)}, f32[4,128,128]{2,1,0:T(8,128)S(1)}, u32[]{:S(2)}, u32[]{:S(2)}) collective-permute-start(f32[4,128,128]{2,1,0:T(8,128)S(1)} %add.370), channel_id=1, source_target_pairs={{0,8},{1,9},{2,10},{3,11},{4,12},{5,13},{6,14},{7,15},{8,0},{9,1},... | collective-permute-start | bytes 786440 | tf_op jit(solution)/shard_map/ppermute | solution.py:14
  73.6 1.0 %fusion.3 = bf16[4,256,128]{2,1,0:T(8,128)(2,1)} fusion(f32[4,256,128]{2,1,0:T(8,128)S(1)} %copy.41, bf16[4,256,256]{1,2,0:T(8,128)(2,1)S(1)} %get-tuple-element.67, bf16[4,256,128]{2,1,0:T(8,128)(2,1)S(1)} %copy-done.1), kind=kOutput, calls=%fused_computation.12 | convolution fusion | flops 67371008 | bytes 1572864 | tf_op jit(solution)/shard_map/hts,hsd->htd/dot_general | solution.py:98
  74.7 5.8 %collective-permute-done.9 = f32[4,128,128]{2,1,0:T(8,128)S(1)} collective-permute-done((f32[4,128,128]{2,1,0:T(8,128)S(1)}, f32[4,128,128]{2,1,0:T(8,128)S(1)}, u32[]{:S(2)}, u32[]{:S(2)}) %collective-permute-start.9) | collective-permute-done | bytes 262176 | tf_op jit(solution)/shard_map/ppermute | solution.py:14
  80.5 3.4 %collective-permute-done.13 = f32[4,128,128]{2,1,0:T(8,128)S(1)} collective-permute-done((f32[4,128,128]{2,1,0:T(8,128)S(1)}, f32[4,128,128]{2,1,0:T(8,128)S(1)}, u32[]{:S(2)}, u32[]{:S(2)}) %collective-permute-start.13) | collective-permute-done | bytes 262176 | tf_op jit(solution)/shard_map/ppermute | solution.py:14
  84.0 1.0 %add_convert_fusion = bf16[4,128,128]{2,1,0:T(8,128)(2,1)S(1)} fusion(f32[4,128,128]{2,1,0:T(8,128)S(1)} %collective-permute-done.13, f32[4,128,128]{2,1,0:T(8,128)S(1)} %collective-permute-done.9, f32[4,128,128]{2,1,0:T(8,128)S(1)} %collective-permute-done.6, f32[4,128,128]{2,1,0:T(8,128)} %collective-permute-done.4, pred[]{:T(512)S(6)} %eq.94, ...), kind=kLoop, calls=%fused_computation.73 | loop fusion | flops 524288 | bytes 1179652 | tf_op jit(solution)/shard_map/convert_element_type | solution.py:116
  85.0 0.9 %fusion.4 = bf16[4,256,128]{2,1,0:T(8,128)(2,1)} fusion(f32[4,256,128]{2,1,0:T(8,128)S(1)} %fusion.41, bf16[4,256,128]{2,1,0:T(8,128)(2,1)S(1)} %copy-done.1, bf16[4,128,128]{2,1,0:T(8,128)(2,1)S(1)} %add_convert_fusion), kind=kOutput, calls=%fused_computation.13 | convolution fusion | flops 33816576 | bytes 1179648 | tf_op jit(solution)/shard_map/hsd,hde->hse/dot_general | solution.py:122
  85.9 0.9 %fusion.5 = bf16[4,256,128]{2,1,0:T(8,128)(2,1)} fusion(f32[4,256,128]{2,1,0:T(8,128)S(1)} %fusion.40, bf16[4,128,128]{2,1,0:T(8,128)(2,1)S(1)} %add_convert_fusion, bf16[4,256,128]{2,1,0:T(8,128)(2,1)S(1)} %copy-done), kind=kOutput, calls=%fused_computation.14 | convolution fusion | flops 33816576 | bytes 1179648 | tf_op jit(solution)/shard_map/hse,hde->hsd/dot_general | solution.py:118
  (116 shorter events, 1.3 us)
Async XLA Ops:
  0.6 7.0 %copy-start.31 = (f32[4,13,256]{2,0,1:T(4,128)S(1)}, f32[4,13,256]{2,0,1:T(4,128)}, u32[]{:S(2)}) copy-start(f32[4,13,256]{2,0,1:T(4,128)} %param.9) | copy-start | bytes 159748
  0.7 16.0 %copy-start.30 = (bf16[4,256,128]{2,1,0:T(8,128)(2,1)S(1)}, bf16[4,256,128]{2,1,0:T(8,128)(2,1)}, u32[]{:S(2)}) copy-start(bf16[4,256,128]{2,1,0:T(8,128)(2,1)} %param.11) | copy-start | bytes 786436
  0.7 16.2 %copy-start.2 = (bf16[4,256,128]{2,1,0:T(8,128)(2,1)S(1)}, bf16[4,256,128]{2,1,0:T(8,128)(2,1)}, u32[]{:S(2)}) copy-start(bf16[4,256,128]{2,1,0:T(8,128)(2,1)} %param.6) | copy-start | bytes 786436
  2.8 1.7 %collective-permute-start = (f32[4,128,128]{2,1,0:T(8,128)S(1)}, f32[4,128,128]{2,1,0:T(8,128)S(1)}, u32[]{:S(2)}, u32[]{:S(2)}) collective-permute-start(f32[4,128,128]{2,1,0:T(8,128)S(1)} %fusion.39), channel_id=1, source_target_pairs={{0,1},{1,0},{2,3},{3,2},{4,5},{5,4},{6,7},{7,6},{8,9},{9,8},{10,11... | collective-permute-start | bytes 786440 | tf_op jit(solution)/shard_map/ppermute | solution.py:14
  3.7 23.6 %copy-start.16 = (pred[256,256]{0,1:T(8,128)(4,1)}, pred[256,256]{0,1:T(8,128)(4,1)S(1)}, u32[]{:S(2)}) copy-start(pred[256,256]{0,1:T(8,128)(4,1)S(1)} %get-tuple-element.71) | copy-start | bytes 196612
  3.7 23.6 %copy-start.18 = (pred[256,256]{0,1:T(8,128)(4,1)}, pred[256,256]{0,1:T(8,128)(4,1)S(1)}, u32[]{:S(2)}) copy-start(pred[256,256]{0,1:T(8,128)(4,1)S(1)} %get-tuple-element.72) | copy-start | bytes 196612
  4.6 31.7 %copy-start.9 = (f32[1,4,128,128]{3,2,1,0:T(8,128)}, f32[1,4,128,128]{3,2,1,0:T(8,128)S(1)}, u32[]{:S(2)}) copy-start(f32[1,4,128,128]{3,2,1,0:T(8,128)S(1)} %get-tuple-element.41) | copy-start | bytes 786436
  4.6 20.7 %copy-start.1 = (bf16[4,256,128]{2,1,0:T(8,128)(2,1)S(1)}, bf16[4,256,128]{2,1,0:T(8,128)(2,1)}, u32[]{:S(2)}) copy-start(bf16[4,256,128]{2,1,0:T(8,128)(2,1)} %param.7) | copy-start | bytes 786436
  4.6 9.5 %collective-permute-start.1 = (f32[4,128,128]{2,1,0:T(8,128)S(1)}, f32[4,128,128]{2,1,0:T(8,128)S(1)}, u32[]{:S(2)}, u32[]{:S(2)}) collective-permute-start(f32[4,128,128]{2,1,0:T(8,128)S(1)} %get-tuple-element.42), channel_id=1, source_target_pairs={{0,2},{1,3},{2,0},{3,1},{4,6},{5,7},{6,4},{7,5},{8,10},{9,11},{10,... | collective-permute-start | bytes 786440 | tf_op jit(solution)/shard_map/ppermute | solution.py:14
  7.6 19.7 %copy-start.20 = (pred[256,256]{0,1:T(8,128)(4,1)}, pred[256,256]{0,1:T(8,128)(4,1)S(1)}, u32[]{:S(2)}) copy-start(pred[256,256]{0,1:T(8,128)(4,1)S(1)} %fusion.28) | copy-start | bytes 196612
  7.7 19.7 %copy-start.33 = (f32[4,256]{1,0:T(4,128)}, f32[4,256]{1,0:T(4,128)S(1)}, u32[]{:S(2)}) copy-start(f32[4,256]{1,0:T(4,128)S(1)} %get-tuple-element.47) | copy-start | bytes 12292
  7.7 19.6 %copy-start.34 = (f32[4,256]{1,0:T(4,128)}, f32[4,256]{1,0:T(4,128)S(1)}, u32[]{:S(2)}) copy-start(f32[4,256]{1,0:T(4,128)S(1)} %get-tuple-element.50) | copy-start | bytes 12292
  7.7 19.6 %copy-start.35 = (f32[4,256]{1,0:T(4,128)}, f32[4,256]{1,0:T(4,128)S(1)}, u32[]{:S(2)}) copy-start(f32[4,256]{1,0:T(4,128)S(1)} %get-tuple-element.51) | copy-start | bytes 12292
  7.7 19.6 %copy-start.36 = (f32[4,256]{1,0:T(4,128)}, f32[4,256]{1,0:T(4,128)S(1)}, u32[]{:S(2)}) copy-start(f32[4,256]{1,0:T(4,128)S(1)} %get-tuple-element.52) | copy-start | bytes 12292
  7.7 19.6 %copy-start.37 = (f32[4,256]{1,0:T(4,128)}, f32[4,256]{1,0:T(4,128)S(1)}, u32[]{:S(2)}) copy-start(f32[4,256]{1,0:T(4,128)S(1)} %get-tuple-element.53) | copy-start | bytes 12292
  7.7 19.6 %copy-start.38 = (f32[4,256]{1,0:T(4,128)}, f32[4,256]{1,0:T(4,128)S(1)}, u32[]{:S(2)}) copy-start(f32[4,256]{1,0:T(4,128)S(1)} %get-tuple-element.54) | copy-start | bytes 12292
  7.8 19.6 %copy-start.39 = (f32[4,256]{1,0:T(4,128)}, f32[4,256]{1,0:T(4,128)S(1)}, u32[]{:S(2)}) copy-start(f32[4,256]{1,0:T(4,128)S(1)} %get-tuple-element.55) | copy-start | bytes 12292
  7.8 19.6 %copy-start.40 = (f32[4,256]{1,0:T(4,128)}, f32[4,256]{1,0:T(4,128)S(1)}, u32[]{:S(2)}) copy-start(f32[4,256]{1,0:T(4,128)S(1)} %get-tuple-element.56) | copy-start | bytes 12292
  7.8 19.6 %copy-start.41 = (f32[4,256]{1,0:T(4,128)}, f32[4,256]{1,0:T(4,128)S(1)}, u32[]{:S(2)}) copy-start(f32[4,256]{1,0:T(4,128)S(1)} %get-tuple-element.57) | copy-start | bytes 12292
  14.9 7.8 %collective-permute-start.2 = (f32[4,128,128]{2,1,0:T(8,128)S(1)}, f32[4,128,128]{2,1,0:T(8,128)S(1)}, u32[]{:S(2)}, u32[]{:S(2)}) collective-permute-start(f32[4,128,128]{2,1,0:T(8,128)S(1)} %get-tuple-element.44), channel_id=1, source_target_pairs={{0,4},{1,5},{2,6},{3,7},{4,0},{5,1},{6,2},{7,3},{8,12},{9,13},{10,... | collective-permute-start | bytes 786440 | tf_op jit(solution)/shard_map/ppermute | solution.py:14
  18.0 9.5 %copy-start.22 = (pred[256,256]{0,1:T(8,128)(4,1)}, pred[256,256]{0,1:T(8,128)(4,1)S(1)}, u32[]{:S(2)}) copy-start(pred[256,256]{0,1:T(8,128)(4,1)S(1)} %get-tuple-element.73) | copy-start | bytes 196612
  18.0 9.5 %copy-start.24 = (pred[256,256]{0,1:T(8,128)(4,1)}, pred[256,256]{0,1:T(8,128)(4,1)S(1)}, u32[]{:S(2)}) copy-start(pred[256,256]{0,1:T(8,128)(4,1)S(1)} %get-tuple-element.74) | copy-start | bytes 196612
  18.1 9.3 %copy-start.26 = (pred[256,256]{0,1:T(8,128)(4,1)}, pred[256,256]{0,1:T(8,128)(4,1)S(1)}, u32[]{:S(2)}) copy-start(pred[256,256]{0,1:T(8,128)(4,1)S(1)} %get-tuple-element.75) | copy-start | bytes 196612
  18.2 9.3 %copy-start.28 = (pred[256,256]{0,1:T(8,128)(4,1)}, pred[256,256]{0,1:T(8,128)(4,1)S(1)}, u32[]{:S(2)}) copy-start(pred[256,256]{0,1:T(8,128)(4,1)S(1)} %get-tuple-element.76) | copy-start | bytes 196612
  22.7 13.6 %copy-start.13 = (f32[1,4,128,128]{3,2,1,0:T(8,128)}, f32[1,4,128,128]{3,2,1,0:T(8,128)S(1)}, u32[]{:S(2)}) copy-start(f32[1,4,128,128]{3,2,1,0:T(8,128)S(1)} %get-tuple-element.45) | copy-start | bytes 786436
  22.7 13.5 %collective-permute-start.3 = (f32[4,128,128]{2,1,0:T(8,128)S(1)}, f32[4,128,128]{2,1,0:T(8,128)S(1)}, u32[]{:S(2)}, u32[]{:S(2)}) collective-permute-start(f32[4,128,128]{2,1,0:T(8,128)S(1)} %get-tuple-element.46), channel_id=1, source_target_pairs={{0,8},{1,9},{2,10},{3,11},{4,12},{5,13},{6,14},{7,15},{8,0},{9,1},... | collective-permute-start | bytes 786440 | tf_op jit(solution)/shard_map/ppermute | solution.py:14
  25.3 10.9 %copy-start.11 = (f32[1,4,128,128]{3,2,1,0:T(8,128)S(1)}, f32[1,4,128,128]{3,2,1,0:T(8,128)}, u32[]{:S(2)}) copy-start(f32[1,4,128,128]{3,2,1,0:T(8,128)} %get-tuple-element.43) | copy-start | bytes 786436
  27.5 9.9 %copy-start.4 = (bf16[4,256,256]{1,2,0:T(8,128)(2,1)}, bf16[4,256,256]{1,2,0:T(8,128)(2,1)S(1)}, u32[]{:S(2)}) copy-start(bf16[4,256,256]{1,2,0:T(8,128)(2,1)S(1)} %get-tuple-element.64) | copy-start | bytes 1572868
  44.9 2.4 %copy-start.6 = (f32[4,256,256]{1,2,0:T(8,128)S(1)}, f32[4,256,256]{1,2,0:T(8,128)}, u32[]{:S(2)}) copy-start(f32[4,256,256]{1,2,0:T(8,128)} %get-tuple-element.65) | copy-start | bytes 3145732
  44.9 2.4 %copy-start.17 = (pred[256,256]{0,1:T(8,128)(4,1)S(1)}, pred[256,256]{0,1:T(8,128)(4,1)}, u32[]{:S(2)}) copy-start(pred[256,256]{0,1:T(8,128)(4,1)} %copy-done.16) | copy-start | bytes 196612
  44.9 2.4 %copy-start.19 = (pred[256,256]{0,1:T(8,128)(4,1)S(1)}, pred[256,256]{0,1:T(8,128)(4,1)}, u32[]{:S(2)}) copy-start(pred[256,256]{0,1:T(8,128)(4,1)} %copy-done.18) | copy-start | bytes 196612
  48.8 5.1 %copy-start.5 = (bf16[4,256,256]{1,2,0:T(8,128)(2,1)S(1)}, bf16[4,256,256]{1,2,0:T(8,128)(2,1)}, u32[]{:S(2)}) copy-start(bf16[4,256,256]{1,2,0:T(8,128)(2,1)} %copy-done.4) | copy-start | bytes 1572868
  49.5 1.5 %collective-permute-start.10 = (f32[4,128,128]{2,1,0:T(8,128)S(1)}, f32[4,128,128]{2,1,0:T(8,128)S(1)}, u32[]{:S(2)}, u32[]{:S(2)}) collective-permute-start(f32[4,128,128]{2,1,0:T(8,128)S(1)} %get-tuple-element.34), channel_id=1, source_target_pairs={{0,1},{1,0},{2,3},{3,2},{4,5},{5,4},{6,7},{7,6},{8,9},{9,8},{10,11... | collective-permute-start | bytes 786440 | tf_op jit(solution)/shard_map/ppermute | solution.py:14
  49.6 1.9 %collective-permute-start.5 = (f32[4,128,128]{2,1,0:T(8,128)S(1)}, f32[4,128,128]{2,1,0:T(8,128)S(1)}, u32[]{:S(2)}, u32[]{:S(2)}) collective-permute-start(f32[4,128,128]{2,1,0:T(8,128)S(1)} %get-tuple-element.36), channel_id=1, source_target_pairs={{0,1},{1,0},{2,3},{3,2},{4,5},{5,4},{6,7},{7,6},{8,9},{9,8},{10,11... | collective-permute-start | bytes 786440 | tf_op jit(solution)/shard_map/ppermute | solution.py:14
  50.1 1.8 %collective-permute-start.7 = (f32[4,128,128]{2,1,0:T(8,128)S(1)}, f32[4,128,128]{2,1,0:T(8,128)S(1)}, u32[]{:S(2)}, u32[]{:S(2)}) collective-permute-start(f32[4,128,128]{2,1,0:T(8,128)S(1)} %get-tuple-element.35), channel_id=1, source_target_pairs={{0,1},{1,0},{2,3},{3,2},{4,5},{5,4},{6,7},{7,6},{8,9},{9,8},{10,11... | collective-permute-start | bytes 786440 | tf_op jit(solution)/shard_map/ppermute | solution.py:14
  50.1 24.6 %collective-permute-start.4 = (f32[4,128,128]{2,1,0:T(8,128)}, f32[4,128,128]{2,1,0:T(8,128)}, u32[]{:S(2)}, u32[]{:S(2)}) collective-permute-start(f32[4,128,128]{2,1,0:T(8,128)} %get-tuple-element.33), channel_id=1, source_target_pairs={{0,1},{1,0},{2,3},{3,2},{4,5},{5,4},{6,7},{7,6},{8,9},{9,8},{10,11... | collective-permute-start | bytes 786440 | tf_op jit(solution)/shard_map/ppermute | solution.py:14
  50.7 11.6 %copy-start.8 = (f32[1,4,128,128]{3,2,1,0:T(8,128)S(1)}, f32[1,4,128,128]{3,2,1,0:T(8,128)}, u32[]{:S(2)}) copy-start(f32[1,4,128,128]{3,2,1,0:T(8,128)} %copy-done.7) | copy-start | bytes 786436
  50.7 11.6 %copy-start.10 = (f32[1,4,128,128]{3,2,1,0:T(8,128)S(1)}, f32[1,4,128,128]{3,2,1,0:T(8,128)}, u32[]{:S(2)}) copy-start(f32[1,4,128,128]{3,2,1,0:T(8,128)} %copy-done.9) | copy-start | bytes 786436
  50.7 11.6 %copy-start.12 = (f32[1,4,128,128]{3,2,1,0:T(8,128)S(1)}, f32[1,4,128,128]{3,2,1,0:T(8,128)}, u32[]{:S(2)}) copy-start(f32[1,4,128,128]{3,2,1,0:T(8,128)} %get-tuple-element.43) | copy-start | bytes 786436
  50.7 11.6 %copy-start.14 = (f32[1,4,128,128]{3,2,1,0:T(8,128)S(1)}, f32[1,4,128,128]{3,2,1,0:T(8,128)}, u32[]{:S(2)}) copy-start(f32[1,4,128,128]{3,2,1,0:T(8,128)} %copy-done.13) | copy-start | bytes 786436
  52.6 9.2 %collective-permute-start.11 = (f32[4,128,128]{2,1,0:T(8,128)S(1)}, f32[4,128,128]{2,1,0:T(8,128)S(1)}, u32[]{:S(2)}, u32[]{:S(2)}) collective-permute-start(f32[4,128,128]{2,1,0:T(8,128)S(1)} %get-tuple-element.38), channel_id=1, source_target_pairs={{0,2},{1,3},{2,0},{3,1},{4,6},{5,7},{6,4},{7,5},{8,10},{9,11},{10,... | collective-permute-start | bytes 786440 | tf_op jit(solution)/shard_map/ppermute | solution.py:14
  53.8 10.3 %copy-start.42 = (f32[4,13,256]{2,0,1:T(4,128)}, f32[4,13,256]{2,0,1:T(4,128)S(1)}, u32[]{:S(2)}) copy-start(f32[4,13,256]{2,0,1:T(4,128)S(1)} %constant_dynamic-update-slice_fusion) | copy-start | bytes 159748
  54.1 14.0 %collective-permute-start.8 = (f32[4,128,128]{2,1,0:T(8,128)S(1)}, f32[4,128,128]{2,1,0:T(8,128)}, u32[]{:S(2)}, u32[]{:S(2)}) collective-permute-start(f32[4,128,128]{2,1,0:T(8,128)S(1)} %get-tuple-element.39), channel_id=1, source_target_pairs={{0,2},{1,3},{2,0},{3,1},{4,6},{5,7},{6,4},{7,5},{8,10},{9,11},{10,... | collective-permute-start | bytes 786440 | tf_op jit(solution)/shard_map/ppermute | solution.py:14
  61.8 8.7 %collective-permute-start.12 = (f32[4,128,128]{2,1,0:T(8,128)S(1)}, f32[4,128,128]{2,1,0:T(8,128)}, u32[]{:S(2)}, u32[]{:S(2)}) collective-permute-start(f32[4,128,128]{2,1,0:T(8,128)S(1)} %add.369), channel_id=1, source_target_pairs={{0,4},{1,5},{2,6},{3,7},{4,0},{5,1},{6,2},{7,3},{8,12},{9,13},{10,... | collective-permute-start | bytes 786440 | tf_op jit(solution)/shard_map/ppermute | solution.py:14
  64.1 2.4 %copy-start.15 = (f32[4,128,128]{2,1,0:T(8,128)S(1)}, f32[4,128,128]{2,1,0:T(8,128)}, u32[]{:S(2)}) copy-start(f32[4,128,128]{2,1,0:T(8,128)} %get-tuple-element.37) | copy-start | bytes 786436
  66.6 8.1 %collective-permute-start.6 = (f32[4,128,128]{2,1,0:T(8,128)S(1)}, f32[4,128,128]{2,1,0:T(8,128)S(1)}, u32[]{:S(2)}, u32[]{:S(2)}) collective-permute-start(f32[4,128,128]{2,1,0:T(8,128)S(1)} %copy-done.15), channel_id=1, source_target_pairs={{0,2},{1,3},{2,0},{3,1},{4,6},{5,7},{6,4},{7,5},{8,10},{9,11},{10,... | collective-permute-start | bytes 786440 | tf_op jit(solution)/shard_map/ppermute | solution.py:14
  69.1 11.4 %collective-permute-start.9 = (f32[4,128,128]{2,1,0:T(8,128)S(1)}, f32[4,128,128]{2,1,0:T(8,128)S(1)}, u32[]{:S(2)}, u32[]{:S(2)}) collective-permute-start(f32[4,128,128]{2,1,0:T(8,128)S(1)} %add.366), channel_id=1, source_target_pairs={{0,4},{1,5},{2,6},{3,7},{4,0},{5,1},{6,2},{7,3},{8,12},{9,13},{10,... | collective-permute-start | bytes 786440 | tf_op jit(solution)/shard_map/ppermute | solution.py:14
  71.5 12.4 %collective-permute-start.13 = (f32[4,128,128]{2,1,0:T(8,128)S(1)}, f32[4,128,128]{2,1,0:T(8,128)S(1)}, u32[]{:S(2)}, u32[]{:S(2)}) collective-permute-start(f32[4,128,128]{2,1,0:T(8,128)S(1)} %add.370), channel_id=1, source_target_pairs={{0,8},{1,9},{2,10},{3,11},{4,12},{5,13},{6,14},{7,15},{8,0},{9,1},... | collective-permute-start | bytes 786440 | tf_op jit(solution)/shard_map/ppermute | solution.py:14
  (9 other events, 17.4 us)
where the time goes:
time: 87.2 us; the launch traced here: 86.8 us
  waiting for transfers between devices  37.5 us (43%)
  starting transfers between devices  16.6 us (19%)
  matrix products  13.5 us (15%)
  other arithmetic  7.87 us (9%)
  local copies, waits for them, and re-layouts  5.16 us (6%)
  blocking collectives  4.91 us (6%)
  between operations  1.32 us (2%)
    ppermute x14, waiting for transfers between devices, from_partner(): return lax.ppermute(value, axis, pairs)  37.5 us
    ppermute x14, starting transfers between devices, from_partner(): return lax.ppermute(value, axis, pairs)  16.6 us
    psum x1, blocking collectives, shards(): totals = lax.psum(jnp.sum(attended * attended, axis=(0, 2)), 'heads')  4.91 us
    add x4, other arithmetic, shards(): level_total = level_total + partner  2.78 us
    dot_general x1, matrix products, shards(): jnp.einsum('hte,hse->hts', grad_out, value_rows, preferred_element_type=j...  2.28 us
    unnamed x88, local copies, waits for them, and re-layouts  2.15 us
    dot_general x1, matrix products, shards(): jnp.einsum('htd,hsd->hts', queries, key_rows, preferred_element_type=jnp....  2.01 us
    dot_general x1, matrix products, shards(): jnp.einsum('hte,mhde->mhtd', grad_wide, states, precision=HIGH)  1.84 us
  transfers between devices with their start and end apart: 14, of which 10 were waited for; matrix products, arithmetic and copies ran while one was open for 14% of the time, Pallas kernels for 0%

commit v1 on v0

--- a/solution.py
+++ b/solution.py
@@ -74,7 +74,9 @@
     query_wide = queries.astype(jnp.float32)
     far_terms = jnp.einsum("htd,mhde->mhte", query_wide, states, precision=HIGH)
     attended = near_out + jnp.sum(far_scale[..., None] * far_terms, 0)
-    totals = lax.psum(jnp.sum(attended * attended, axis=(0, 2)), "heads")
+    x = jnp.sum(attended * attended, axis=(0, 2))
+    parts = lax.all_gather(x, "heads", axis=0, tiled=False)
+    totals = parts.sum(axis=0)
     inv_rms = lax.rsqrt(totals / width + EPS)
     normed = (attended * inv_rms[None, :, None] * norm_gain[:, None, :]).astype(jnp.bfloat16)
     scaled = norm_gain[:, None, :] * grad_normed.astype(jnp.float32)

time: 87.2 us -> 91.5 us (1.049)
  blocking collectives: 4.91 us -> 9.14 us
    all_gather x0 -> x1, blocking collectives: none -> 4.23 us  [shards(): parts = lax.all_gather(x, 'heads', axis=0, tiled=False)]
where the time goes in v1:
time: 91.5 us; the launch traced here: 91.1 us
  waiting for transfers between devices  37.5 us (41%)
  starting transfers between devices  16.5 us (18%)
  matrix products  13.6 us (15%)
  blocking collectives  9.14 us (10%)
  other arithmetic  7.91 us (9%)
  local copies, waits for them, and re-layouts  5.18 us (6%)
  between operations  1.33 us (1%)
    ppermute x14, waiting for transfers between devices, from_partner(): return lax.ppermute(value, axis, pairs)  37.5 us
    ppermute x14, starting transfers between devices, from_partner(): return lax.ppermute(value, axis, pairs)  16.5 us
    psum x1, blocking collectives, shards(): inner_sum = lax.psum(jnp.sum(scaled * attended, axis=(0, 2)), 'heads')  4.91 us
    all_gather x1, blocking collectives, shards(): parts = lax.all_gather(x, 'heads', axis=0, tiled=False)  4.23 us
    add x4, other arithmetic, shards(): level_total = level_total + partner  2.8 us
    dot_general x1, matrix products, shards(): jnp.einsum('hte,hse->hts', grad_out, value_rows, preferred_element_type=j...  2.29 us
    unnamed x88, local copies, waits for them, and re-layouts  2.15 us
    dot_general x1, matrix products, shards(): jnp.einsum('htd,hsd->hts', queries, key_rows, preferred_element_type=jnp....  2.01 us
  transfers between devices with their start and end apart: 14, of which 10 were waited for; matrix products, arithmetic and copies ran while one was open for 14% of the time, Pallas kernels for 0%

profile of v1, /device:TPU:0, one launch (start us, length us, event | category | flops | bytes accessed | tf_op | source)
XLA Modules:
  0.0 91.1 jit_solution(14427903694990783664)
XLA Ops:
  0.7 0.9 %copy-done = bf16[4,256,128]{2,1,0:T(8,128)(2,1)S(1)} copy-done((bf16[4,256,128]{2,1,0:T(8,128)(2,1)S(1)}, bf16[4,256,128]{2,1,0:T(8,128)(2,1)}, u32[]{:S(2)}) %copy-start) | copy-done | bytes 262168
  1.6 1.2 %fusion.39 = f32[4,128,128]{2,1,0:T(8,128)S(1)} fusion(bf16[4,256,128]{2,1,0:T(8,128)(2,1)} %param.7, bf16[4,256,128]{2,1,0:T(8,128)(2,1)S(1)} %copy-done), kind=kOutput, calls=%fused_computation.115 | convolution fusion | flops 33554432 | bytes 786432 | tf_op jit(solution)/shard_map/hsd,hse->hde/dot_general | solution.py:51
  2.8 0.6 collective-permute-start
  3.7 0.8 collective-permute-done
  4.6 2.9 %collective-permute-start.1 = (f32[4,128,128]{2,1,0:T(8,128)S(1)}, f32[4,128,128]{2,1,0:T(8,128)S(1)}, u32[]{:S(2)}, u32[]{:S(2)}) collective-permute-start(f32[4,128,128]{2,1,0:T(8,128)S(1)} %get-tuple-element.40), channel_id=1, source_target_pairs={{0,2},{1,3},{2,0},{3,1},{4,6},{5,7},{6,4},{7,5},{8,10},{9,11},{10,... | collective-permute-start | bytes 786440 | tf_op jit(solution)/shard_map/ppermute | solution.py:14
  7.8 6.3 %collective-permute-done.1 = f32[4,128,128]{2,1,0:T(8,128)S(1)} collective-permute-done((f32[4,128,128]{2,1,0:T(8,128)S(1)}, f32[4,128,128]{2,1,0:T(8,128)S(1)}, u32[]{:S(2)}, u32[]{:S(2)}) %collective-permute-start.1) | collective-permute-done | bytes 262176 | tf_op jit(solution)/shard_map/ppermute | solution.py:14
  14.1 0.7 select_bitcast_fusion.2
  14.9 1.8 %collective-permute-start.2 = (f32[4,128,128]{2,1,0:T(8,128)S(1)}, f32[4,128,128]{2,1,0:T(8,128)S(1)}, u32[]{:S(2)}, u32[]{:S(2)}) collective-permute-start(f32[4,128,128]{2,1,0:T(8,128)S(1)} %get-tuple-element.42), channel_id=1, source_target_pairs={{0,4},{1,5},{2,6},{3,7},{4,0},{5,1},{6,2},{7,3},{8,12},{9,13},{10,... | collective-permute-start | bytes 786440 | tf_op jit(solution)/shard_map/ppermute | solution.py:14
  16.9 1.0 %copy.42 = f32[4,256,128]{1,2,0:T(8,128)} copy(bf16[4,256,128]{2,1,0:T(8,128)(2,1)S(1)} %copy-done.2) | data formatting | bytes 786432 | tf_op jit(solution)/shard_map/convert_element_type | solution.py:104
  18.2 4.4 %collective-permute-done.2 = f32[4,128,128]{2,1,0:T(8,128)S(1)} collective-permute-done((f32[4,128,128]{2,1,0:T(8,128)S(1)}, f32[4,128,128]{2,1,0:T(8,128)S(1)}, u32[]{:S(2)}, u32[]{:S(2)}) %collective-permute-start.2) | collective-permute-done | bytes 262176 | tf_op jit(solution)/shard_map/ppermute | solution.py:14
  22.7 2.6 %collective-permute-start.3 = (f32[4,128,128]{2,1,0:T(8,128)S(1)}, f32[4,128,128]{2,1,0:T(8,128)S(1)}, u32[]{:S(2)}, u32[]{:S(2)}) collective-permute-start(f32[4,128,128]{2,1,0:T(8,128)S(1)} %get-tuple-element.44), channel_id=1, source_target_pairs={{0,8},{1,9},{2,10},{3,11},{4,12},{5,13},{6,14},{7,15},{8,0},{9,1},... | collective-permute-start | bytes 786440 | tf_op jit(solution)/shard_map/ppermute | solution.py:14
  25.3 2.0 %multiply_convert_fusion.3 = (bf16[4,256,256]{1,2,0:T(8,128)(2,1)S(1)}, f32[4,256,256]{1,2,0:T(8,128)}) fusion(f32[4,256]{1,0:T(4,128)S(1)} %get-tuple-element.48, pred[256,256]{0,1:T(8,128)(4,1)S(1)} %get-tuple-element.67, f32[4,256]{1,0:T(4,128)S(1)} %get-tuple-element.49, pred[256,256]{0,1:T(8,128)(4,1)S(1)} %get-tuple-element.68, ...), kind=kOutput, calls=%fused_computation.28 | convolution fusion | flops 72089600 | bytes 2723840 | tf_op jit(solution)/shard_map/htd,hsd->hts/dot_general | solution.py:64
  27.5 8.7 %collective-permute-done.3 = f32[4,128,128]{2,1,0:T(8,128)S(1)} collective-permute-done((f32[4,128,128]{2,1,0:T(8,128)S(1)}, f32[4,128,128]{2,1,0:T(8,128)S(1)}, u32[]{:S(2)}, u32[]{:S(2)}) %collective-permute-start.3) | collective-permute-done | bytes 262176 | tf_op jit(solution)/shard_map/ppermute | solution.py:14
  36.3 1.1 %multiply_reduce_fusion = (f32[4,256,128]{1,2,0:T(8,128)S(1)}, f32[4,4,256,128]{2,3,1,0:T(8,128)S(1)}) fusion(f32[4,4,256]{2,1,0:T(4,128)S(1)} %pad_maximum_fusion.3, bf16[4,256,128]{2,1,0:T(8,128)(2,1)S(1)} %copy-done.2, f32[1,4,128,128]{3,2,1,0:T(8,128)S(1)} %select_bitcast_fusion, f32[1,4,128,128]{3,2,1,0:T(8,128)S(1)} %get-tuple-element.43, ...), kind=kOutput, calls=%fused_computation.3 | convolution fusion | flops 807010304 | bytes 3948544 | tf_op jit(solution)/shard_map/htd,mhde->mhte/dot_general | solution.py:75
  37.4 1.1 %multiply_reduce_fusion.1 = (f32[256]{0:T(256)S(1)}, f32[256]{0:T(256)S(1)}, f32[4,256,128]{1,2,0:T(8,128)}) fusion(bf16[4,256,128]{1,2,0:T(8,128)(2,1)S(1)} %copy.35, f32[4,128]{1,0:T(4,128)S(1)} %copy-done.32, f32[4,256,128]{1,2,0:T(8,128)S(1)} %get-tuple-element.60, bf16[4,256,256]{1,2,0:T(8,128)(2,1)S(1)} %get-tuple-element.62, ...), kind=kOutput, calls=%fused_computation.43 | convolution fusion | flops 68025856 | bytes 2101248 | tf_op jit(solution)/shard_map/hts,hse->hte/dot_general | solution.py:66
  38.6 4.2 %all-gather.1 = f32[2,1,256]{2,1,0:T(1,128)S(1)} all-gather(f32[1,1,256]{2,1,0:T(1,128)S(1)} %bitcast.140), channel_id=2, replica_groups=mesh['heads'=2,'ctx'=16] {'heads'}, dimensions={0}, use_global_device_ids=true | all-gather | bytes 3072 | tf_op jit(solution)/shard_map/all_gather | solution.py:78
  42.8 4.9 %psum.7 = f32[256]{0:T(256)S(1)} all-reduce(f32[256]{0:T(256)S(1)} %get-tuple-element.28), channel_id=1, replica_groups=mesh['heads'=2,'ctx'=16] {'heads'}, use_global_device_ids=true, to_apply=%region_4.5 | all-reduce | flops 256 | bytes 2048 | tf_op jit(solution)/shard_map/psum | solution.py:83
  47.8 1.4 %fusion.11 = (f32[4,256]{1,0:T(4,128)S(1)}, f32[4,256]{1,0:T(4,128)S(1)}, f32[4,256]{1,0:T(4,128)S(1)}, f32[4,256]{1,0:T(4,128)S(1)}, bf16[4,256,128]{1,2,0:T(8,128)(2,1)S(1)}, /*index=5*/bf16[4,256,128]{1,2,0:T(8,128)(2,1)S(1)}) fusion(f32[4,4,256,128]{2,3,1,0:T(8,128)S(1)} %get-tuple-element.61, f32[4,256,128]{1,2,0:T(8,128)} %get-tuple-element.64, ...), kind=kLoop, calls=%fused_computation.37 | loop fusion | flops 2355200 | bytes 3428352 | tf_op jit(solution)/shard_map/reduce_sum | solution.py:96
  49.3 2.3 %multiply_convert_fusion.2 = (bf16[4,256,256]{1,2,0:T(8,128)(2,1)S(1)}, f32[4,256,256]{1,2,0:T(8,128)S(1)}) fusion(f32[4,256]{1,0:T(4,128)} %copy-done.34, pred[256,256]{0,1:T(8,128)(4,1)S(1)} %get-tuple-element.67, f32[4,256]{1,0:T(4,128)} %copy-done.35, pred[256,256]{0,1:T(8,128)(4,1)S(1)} %get-tuple-element.68, f32[4,256]{1,0:T(4,128)} %copy-done.36, ...), kind=kOutput, calls=%fused_computation.26 | convolution fusion | flops 72089600 | bytes 2723840 | tf_op jit(solution)/shard_map/hte,hse->hts/dot_general | solution.py:88
  51.6 0.9 select_reduce_fusion
  52.6 0.4 convolution_bitcast_fusion.1
  53.0 0.8 slice_bitcast_fusion.7
  53.8 0.5 collective-permute-start.5
  54.3 0.5 collective-permute-start.4
  55.0 0.4 collective-permute-done.10
  55.4 0.4 collective-permute-done.5
  55.7 0.4 collective-permute-done.7
  56.1 0.8 fusion.36
  56.9 1.2 %collective-permute-start.11 = (f32[4,128,128]{2,1,0:T(8,128)S(1)}, f32[4,128,128]{2,1,0:T(8,128)S(1)}, u32[]{:S(2)}, u32[]{:S(2)}) collective-permute-start(f32[4,128,128]{2,1,0:T(8,128)S(1)} %get-tuple-element.36), channel_id=1, source_target_pairs={{0,2},{1,3},{2,0},{3,1},{4,6},{5,7},{6,4},{7,5},{8,10},{9,11},{10,... | collective-permute-start | bytes 786440 | tf_op jit(solution)/shard_map/ppermute | solution.py:14
  58.1 0.3 fusion.41
  58.4 0.9 %collective-permute-start.8 = (f32[4,128,128]{2,1,0:T(8,128)S(1)}, f32[4,128,128]{2,1,0:T(8,128)}, u32[]{:S(2)}, u32[]{:S(2)}) collective-permute-start(f32[4,128,128]{2,1,0:T(8,128)S(1)} %get-tuple-element.37), channel_id=1, source_target_pairs={{0,2},{1,3},{2,0},{3,1},{4,6},{5,7},{6,4},{7,5},{8,10},{9,11},{10,... | collective-permute-start | bytes 786440 | tf_op jit(solution)/shard_map/ppermute | solution.py:14
  59.3 6.8 %collective-permute-done.11 = f32[4,128,128]{2,1,0:T(8,128)S(1)} collective-permute-done((f32[4,128,128]{2,1,0:T(8,128)S(1)}, f32[4,128,128]{2,1,0:T(8,128)S(1)}, u32[]{:S(2)}, u32[]{:S(2)}) %collective-permute-start.11) | collective-permute-done | bytes 262176 | tf_op jit(solution)/shard_map/ppermute | solution.py:14
  66.1 0.4 collective-permute-start.12
  66.6 1.8 %fusion = f32[4,256,128]{1,2,0:T(8,128)} fusion(f32[4,4,256]{2,1,0:T(4,128)S(1)} %pad_maximum_fusion.3, f32[1,4,128,128]{3,2,1,0:T(8,128)S(1)} %copy-done.8, f32[1,4,128,128]{3,2,1,0:T(8,128)S(1)} %copy-done.14, f32[1,4,128,128]{3,2,1,0:T(8,128)S(1)} %copy-done.12, f32[1,4,128,128]{3,2,1,0:T(8,128)S(1)} %copy-done.10, ...), kind=kOutput, calls=%fused_computation.1 | convolution fusion | flops 807010304 | bytes 1851392 | tf_op jit(solution)/shard_map/hte,mhde->mhtd/dot_general | solution.py:102
  68.4 1.3 %copy.41 = f32[4,256,128]{2,1,0:T(8,128)S(1)} copy(f32[4,256,128]{1,2,0:T(8,128)} %fusion) | data formatting | bytes 1048576 | tf_op jit(solution)/shard_map/reduce_sum | solution.py:101
  69.7 0.8 copy.49
  70.5 0.3 fusion.40
  70.8 1.6 %collective-permute-start.6 = (f32[4,128,128]{2,1,0:T(8,128)S(1)}, f32[4,128,128]{2,1,0:T(8,128)S(1)}, u32[]{:S(2)}, u32[]{:S(2)}) collective-permute-start(f32[4,128,128]{2,1,0:T(8,128)S(1)} %copy-done.15), channel_id=1, source_target_pairs={{0,2},{1,3},{2,0},{3,1},{4,6},{5,7},{6,4},{7,5},{8,10},{9,11},{10,... | collective-permute-start | bytes 786440 | tf_op jit(solution)/shard_map/ppermute | solution.py:14
  72.4 1.0 %add.368 = f32[4,128,128]{2,1,0:T(8,128)S(1)} add(f32[4,128,128]{2,1,0:T(8,128)S(1)} %get-tuple-element.37, f32[4,128,128]{2,1,0:T(8,128)} %collective-permute-done.8) | non-fusion elementwise | flops 65536 | bytes 786432 | tf_op jit(solution)/shard_map/add | solution.py:114
  73.4 1.4 %collective-permute-start.9 = (f32[4,128,128]{2,1,0:T(8,128)S(1)}, f32[4,128,128]{2,1,0:T(8,128)S(1)}, u32[]{:S(2)}, u32[]{:S(2)}) collective-permute-start(f32[4,128,128]{2,1,0:T(8,128)S(1)} %add.368), channel_id=1, source_target_pairs={{0,4},{1,5},{2,6},{3,7},{4,0},{5,1},{6,2},{7,3},{8,12},{9,13},{10,... | collective-permute-start | bytes 786440 | tf_op jit(solution)/shard_map/ppermute | solution.py:14
  74.8 1.0 %add.372 = f32[4,128,128]{2,1,0:T(8,128)S(1)} add(f32[4,128,128]{2,1,0:T(8,128)S(1)} %add.371, f32[4,128,128]{2,1,0:T(8,128)} %collective-permute-done.12) | non-fusion elementwise | flops 65536 | bytes 786432 | tf_op jit(solution)/shard_map/add | solution.py:114
  75.8 2.1 %collective-permute-start.13 = (f32[4,128,128]{2,1,0:T(8,128)S(1)}, f32[4,128,128]{2,1,0:T(8,128)S(1)}, u32[]{:S(2)}, u32[]{:S(2)}) collective-permute-start(f32[4,128,128]{2,1,0:T(8,128)S(1)} %add.372), channel_id=1, source_target_pairs={{0,8},{1,9},{2,10},{3,11},{4,12},{5,13},{6,14},{7,15},{8,0},{9,1},... | collective-permute-start | bytes 786440 | tf_op jit(solution)/shard_map/ppermute | solution.py:14
  77.9 1.1 %fusion.3 = bf16[4,256,128]{2,1,0:T(8,128)(2,1)} fusion(f32[4,256,128]{2,1,0:T(8,128)S(1)} %copy.41, bf16[4,256,256]{1,2,0:T(8,128)(2,1)S(1)} %get-tuple-element.65, bf16[4,256,128]{2,1,0:T(8,128)(2,1)S(1)} %copy-done.1), kind=kOutput, calls=%fused_computation.12 | convolution fusion | flops 67371008 | bytes 1572864 | tf_op jit(solution)/shard_map/hts,hsd->htd/dot_general | solution.py:100
  79.0 5.8 %collective-permute-done.9 = f32[4,128,128]{2,1,0:T(8,128)S(1)} collective-permute-done((f32[4,128,128]{2,1,0:T(8,128)S(1)}, f32[4,128,128]{2,1,0:T(8,128)S(1)}, u32[]{:S(2)}, u32[]{:S(2)}) %collective-permute-start.9) | collective-permute-done | bytes 262176 | tf_op jit(solution)/shard_map/ppermute | solution.py:14
  84.8 3.4 %collective-permute-done.13 = f32[4,128,128]{2,1,0:T(8,128)S(1)} collective-permute-done((f32[4,128,128]{2,1,0:T(8,128)S(1)}, f32[4,128,128]{2,1,0:T(8,128)S(1)}, u32[]{:S(2)}, u32[]{:S(2)}) %collective-permute-start.13) | collective-permute-done | bytes 262176 | tf_op jit(solution)/shard_map/ppermute | solution.py:14
  88.2 1.0 %add_convert_fusion = bf16[4,128,128]{2,1,0:T(8,128)(2,1)S(1)} fusion(f32[4,128,128]{2,1,0:T(8,128)S(1)} %collective-permute-done.13, f32[4,128,128]{2,1,0:T(8,128)S(1)} %collective-permute-done.9, f32[4,128,128]{2,1,0:T(8,128)S(1)} %collective-permute-done.6, f32[4,128,128]{2,1,0:T(8,128)} %collective-permute-done.4, pred[]{:T(512)S(6)} %eq.94, ...), kind=kLoop, calls=%fused_computation.73 | loop fusion | flops 524288 | bytes 1179652 | tf_op jit(solution)/shard_map/convert_element_type | solution.py:118
  89.2 0.9 %fusion.4 = bf16[4,256,128]{2,1,0:T(8,128)(2,1)} fusion(f32[4,256,128]{2,1,0:T(8,128)S(1)} %fusion.41, bf16[4,256,128]{2,1,0:T(8,128)(2,1)S(1)} %copy-done.1, bf16[4,128,128]{2,1,0:T(8,128)(2,1)S(1)} %add_convert_fusion), kind=kOutput, calls=%fused_computation.13 | convolution fusion | flops 33816576 | bytes 1179648 | tf_op jit(solution)/shard_map/hsd,hde->hse/dot_general | solution.py:124
  90.2 0.9 %fusion.5 = bf16[4,256,128]{2,1,0:T(8,128)(2,1)} fusion(f32[4,256,128]{2,1,0:T(8,128)S(1)} %fusion.40, bf16[4,128,128]{2,1,0:T(8,128)(2,1)S(1)} %add_convert_fusion, bf16[4,256,128]{2,1,0:T(8,128)(2,1)S(1)} %copy-done), kind=kOutput, calls=%fused_computation.14 | convolution fusion | flops 33816576 | bytes 1179648 | tf_op jit(solution)/shard_map/hse,hde->hsd/dot_general | solution.py:120
  (118 shorter events, 1.5 us)
Async XLA Ops:
  0.6 7.0 %copy-start.31 = (f32[4,13,256]{2,0,1:T(4,128)S(1)}, f32[4,13,256]{2,0,1:T(4,128)}, u32[]{:S(2)}) copy-start(f32[4,13,256]{2,0,1:T(4,128)} %param.9) | copy-start | bytes 159748
  0.7 16.0 %copy-start.30 = (bf16[4,256,128]{2,1,0:T(8,128)(2,1)S(1)}, bf16[4,256,128]{2,1,0:T(8,128)(2,1)}, u32[]{:S(2)}) copy-start(bf16[4,256,128]{2,1,0:T(8,128)(2,1)} %param.11) | copy-start | bytes 786436
  0.7 16.2 %copy-start.2 = (bf16[4,256,128]{2,1,0:T(8,128)(2,1)S(1)}, bf16[4,256,128]{2,1,0:T(8,128)(2,1)}, u32[]{:S(2)}) copy-start(bf16[4,256,128]{2,1,0:T(8,128)(2,1)} %param.6) | copy-start | bytes 786436
  2.8 1.7 %collective-permute-start = (f32[4,128,128]{2,1,0:T(8,128)S(1)}, f32[4,128,128]{2,1,0:T(8,128)S(1)}, u32[]{:S(2)}, u32[]{:S(2)}) collective-permute-start(f32[4,128,128]{2,1,0:T(8,128)S(1)} %fusion.39), channel_id=1, source_target_pairs={{0,1},{1,0},{2,3},{3,2},{4,5},{5,4},{6,7},{7,6},{8,9},{9,8},{10,11... | collective-permute-start | bytes 786440 | tf_op jit(solution)/shard_map/ppermute | solution.py:14
  3.7 23.6 %copy-start.16 = (pred[256,256]{0,1:T(8,128)(4,1)}, pred[256,256]{0,1:T(8,128)(4,1)S(1)}, u32[]{:S(2)}) copy-start(pred[256,256]{0,1:T(8,128)(4,1)S(1)} %get-tuple-element.69) | copy-start | bytes 196612
  3.7 23.6 %copy-start.18 = (pred[256,256]{0,1:T(8,128)(4,1)}, pred[256,256]{0,1:T(8,128)(4,1)S(1)}, u32[]{:S(2)}) copy-start(pred[256,256]{0,1:T(8,128)(4,1)S(1)} %get-tuple-element.70) | copy-start | bytes 196612
  4.6 31.7 %copy-start.9 = (f32[1,4,128,128]{3,2,1,0:T(8,128)}, f32[1,4,128,128]{3,2,1,0:T(8,128)S(1)}, u32[]{:S(2)}) copy-start(f32[1,4,128,128]{3,2,1,0:T(8,128)S(1)} %get-tuple-element.39) | copy-start | bytes 786436
  4.6 20.7 %copy-start.1 = (bf16[4,256,128]{2,1,0:T(8,128)(2,1)S(1)}, bf16[4,256,128]{2,1,0:T(8,128)(2,1)}, u32[]{:S(2)}) copy-start(bf16[4,256,128]{2,1,0:T(8,128)(2,1)} %param.7) | copy-start | bytes 786436
  4.6 9.5 %collective-permute-start.1 = (f32[4,128,128]{2,1,0:T(8,128)S(1)}, f32[4,128,128]{2,1,0:T(8,128)S(1)}, u32[]{:S(2)}, u32[]{:S(2)}) collective-permute-start(f32[4,128,128]{2,1,0:T(8,128)S(1)} %get-tuple-element.40), channel_id=1, source_target_pairs={{0,2},{1,3},{2,0},{3,1},{4,6},{5,7},{6,4},{7,5},{8,10},{9,11},{10,... | collective-permute-start | bytes 786440 | tf_op jit(solution)/shard_map/ppermute | solution.py:14
  7.6 19.7 %copy-start.20 = (pred[256,256]{0,1:T(8,128)(4,1)}, pred[256,256]{0,1:T(8,128)(4,1)S(1)}, u32[]{:S(2)}) copy-start(pred[256,256]{0,1:T(8,128)(4,1)S(1)} %fusion.28) | copy-start | bytes 196612
  7.7 19.7 %copy-start.33 = (f32[4,256]{1,0:T(4,128)}, f32[4,256]{1,0:T(4,128)S(1)}, u32[]{:S(2)}) copy-start(f32[4,256]{1,0:T(4,128)S(1)} %get-tuple-element.45) | copy-start | bytes 12292
  7.7 19.6 %copy-start.34 = (f32[4,256]{1,0:T(4,128)}, f32[4,256]{1,0:T(4,128)S(1)}, u32[]{:S(2)}) copy-start(f32[4,256]{1,0:T(4,128)S(1)} %get-tuple-element.48) | copy-start | bytes 12292
  7.7 19.6 %copy-start.35 = (f32[4,256]{1,0:T(4,128)}, f32[4,256]{1,0:T(4,128)S(1)}, u32[]{:S(2)}) copy-start(f32[4,256]{1,0:T(4,128)S(1)} %get-tuple-element.49) | copy-start | bytes 12292
  7.7 19.6 %copy-start.36 = (f32[4,256]{1,0:T(4,128)}, f32[4,256]{1,0:T(4,128)S(1)}, u32[]{:S(2)}) copy-start(f32[4,256]{1,0:T(4,128)S(1)} %get-tuple-element.50) | copy-start | bytes 12292
  7.7 19.6 %copy-start.37 = (f32[4,256]{1,0:T(4,128)}, f32[4,256]{1,0:T(4,128)S(1)}, u32[]{:S(2)}) copy-start(f32[4,256]{1,0:T(4,128)S(1)} %get-tuple-element.51) | copy-start | bytes 12292
  7.7 19.6 %copy-start.38 = (f32[4,256]{1,0:T(4,128)}, f32[4,256]{1,0:T(4,128)S(1)}, u32[]{:S(2)}) copy-start(f32[4,256]{1,0:T(4,128)S(1)} %get-tuple-element.52) | copy-start | bytes 12292
  7.8 19.6 %copy-start.39 = (f32[4,256]{1,0:T(4,128)}, f32[4,256]{1,0:T(4,128)S(1)}, u32[]{:S(2)}) copy-start(f32[4,256]{1,0:T(4,128)S(1)} %get-tuple-element.53) | copy-start | bytes 12292
  7.8 19.6 %copy-start.40 = (f32[4,256]{1,0:T(4,128)}, f32[4,256]{1,0:T(4,128)S(1)}, u32[]{:S(2)}) copy-start(f32[4,256]{1,0:T(4,128)S(1)} %get-tuple-element.54) | copy-start | bytes 12292
  7.8 19.6 %copy-start.41 = (f32[4,256]{1,0:T(4,128)}, f32[4,256]{1,0:T(4,128)S(1)}, u32[]{:S(2)}) copy-start(f32[4,256]{1,0:T(4,128)S(1)} %get-tuple-element.55) | copy-start | bytes 12292
  14.9 7.8 %collective-permute-start.2 = (f32[4,128,128]{2,1,0:T(8,128)S(1)}, f32[4,128,128]{2,1,0:T(8,128)S(1)}, u32[]{:S(2)}, u32[]{:S(2)}) collective-permute-start(f32[4,128,128]{2,1,0:T(8,128)S(1)} %get-tuple-element.42), channel_id=1, source_target_pairs={{0,4},{1,5},{2,6},{3,7},{4,0},{5,1},{6,2},{7,3},{8,12},{9,13},{10,... | collective-permute-start | bytes 786440 | tf_op jit(solution)/shard_map/ppermute | solution.py:14
  18.0 9.4 %copy-start.22 = (pred[256,256]{0,1:T(8,128)(4,1)}, pred[256,256]{0,1:T(8,128)(4,1)S(1)}, u32[]{:S(2)}) copy-start(pred[256,256]{0,1:T(8,128)(4,1)S(1)} %get-tuple-element.71) | copy-start | bytes 196612
  18.0 9.4 %copy-start.24 = (pred[256,256]{0,1:T(8,128)(4,1)}, pred[256,256]{0,1:T(8,128)(4,1)S(1)}, u32[]{:S(2)}) copy-start(pred[256,256]{0,1:T(8,128)(4,1)S(1)} %get-tuple-element.72) | copy-start | bytes 196612
  18.2 9.3 %copy-start.26 = (pred[256,256]{0,1:T(8,128)(4,1)}, pred[256,256]{0,1:T(8,128)(4,1)S(1)}, u32[]{:S(2)}) copy-start(pred[256,256]{0,1:T(8,128)(4,1)S(1)} %get-tuple-element.73) | copy-start | bytes 196612
  18.2 9.3 %copy-start.28 = (pred[256,256]{0,1:T(8,128)(4,1)}, pred[256,256]{0,1:T(8,128)(4,1)S(1)}, u32[]{:S(2)}) copy-start(pred[256,256]{0,1:T(8,128)(4,1)S(1)} %get-tuple-element.74) | copy-start | bytes 196612
  22.7 13.6 %copy-start.13 = (f32[1,4,128,128]{3,2,1,0:T(8,128)}, f32[1,4,128,128]{3,2,1,0:T(8,128)S(1)}, u32[]{:S(2)}) copy-start(f32[1,4,128,128]{3,2,1,0:T(8,128)S(1)} %get-tuple-element.43) | copy-start | bytes 786436
  22.7 13.5 %collective-permute-start.3 = (f32[4,128,128]{2,1,0:T(8,128)S(1)}, f32[4,128,128]{2,1,0:T(8,128)S(1)}, u32[]{:S(2)}, u32[]{:S(2)}) collective-permute-start(f32[4,128,128]{2,1,0:T(8,128)S(1)} %get-tuple-element.44), channel_id=1, source_target_pairs={{0,8},{1,9},{2,10},{3,11},{4,12},{5,13},{6,14},{7,15},{8,0},{9,1},... | collective-permute-start | bytes 786440 | tf_op jit(solution)/shard_map/ppermute | solution.py:14
  25.3 10.9 %copy-start.11 = (f32[1,4,128,128]{3,2,1,0:T(8,128)S(1)}, f32[1,4,128,128]{3,2,1,0:T(8,128)}, u32[]{:S(2)}) copy-start(f32[1,4,128,128]{3,2,1,0:T(8,128)} %get-tuple-element.41) | copy-start | bytes 786436
  27.5 9.9 %copy-start.4 = (bf16[4,256,256]{1,2,0:T(8,128)(2,1)}, bf16[4,256,256]{1,2,0:T(8,128)(2,1)S(1)}, u32[]{:S(2)}) copy-start(bf16[4,256,256]{1,2,0:T(8,128)(2,1)S(1)} %get-tuple-element.62) | copy-start | bytes 1572868
  49.2 2.4 %copy-start.6 = (f32[4,256,256]{1,2,0:T(8,128)S(1)}, f32[4,256,256]{1,2,0:T(8,128)}, u32[]{:S(2)}) copy-start(f32[4,256,256]{1,2,0:T(8,128)} %get-tuple-element.63) | copy-start | bytes 3145732
  49.2 2.4 %copy-start.17 = (pred[256,256]{0,1:T(8,128)(4,1)S(1)}, pred[256,256]{0,1:T(8,128)(4,1)}, u32[]{:S(2)}) copy-start(pred[256,256]{0,1:T(8,128)(4,1)} %copy-done.16) | copy-start | bytes 196612
  49.2 2.4 %copy-start.19 = (pred[256,256]{0,1:T(8,128)(4,1)S(1)}, pred[256,256]{0,1:T(8,128)(4,1)}, u32[]{:S(2)}) copy-start(pred[256,256]{0,1:T(8,128)(4,1)} %copy-done.18) | copy-start | bytes 196612
  53.0 5.1 %copy-start.5 = (bf16[4,256,256]{1,2,0:T(8,128)(2,1)S(1)}, bf16[4,256,256]{1,2,0:T(8,128)(2,1)}, u32[]{:S(2)}) copy-start(bf16[4,256,256]{1,2,0:T(8,128)(2,1)} %copy-done.4) | copy-start | bytes 1572868
  53.8 1.5 %collective-permute-start.10 = (f32[4,128,128]{2,1,0:T(8,128)S(1)}, f32[4,128,128]{2,1,0:T(8,128)S(1)}, u32[]{:S(2)}, u32[]{:S(2)}) collective-permute-start(f32[4,128,128]{2,1,0:T(8,128)S(1)} %get-tuple-element.32), channel_id=1, source_target_pairs={{0,1},{1,0},{2,3},{3,2},{4,5},{5,4},{6,7},{7,6},{8,9},{9,8},{10,11... | collective-permute-start | bytes 786440 | tf_op jit(solution)/shard_map/ppermute | solution.py:14
  53.8 1.9 %collective-permute-start.5 = (f32[4,128,128]{2,1,0:T(8,128)S(1)}, f32[4,128,128]{2,1,0:T(8,128)S(1)}, u32[]{:S(2)}, u32[]{:S(2)}) collective-permute-start(f32[4,128,128]{2,1,0:T(8,128)S(1)} %get-tuple-element.34), channel_id=1, source_target_pairs={{0,1},{1,0},{2,3},{3,2},{4,5},{5,4},{6,7},{7,6},{8,9},{9,8},{10,11... | collective-permute-start | bytes 786440 | tf_op jit(solution)/shard_map/ppermute | solution.py:14
  54.3 1.8 %collective-permute-start.7 = (f32[4,128,128]{2,1,0:T(8,128)S(1)}, f32[4,128,128]{2,1,0:T(8,128)S(1)}, u32[]{:S(2)}, u32[]{:S(2)}) collective-permute-start(f32[4,128,128]{2,1,0:T(8,128)S(1)} %get-tuple-element.33), channel_id=1, source_target_pairs={{0,1},{1,0},{2,3},{3,2},{4,5},{5,4},{6,7},{7,6},{8,9},{9,8},{10,11... | collective-permute-start | bytes 786440 | tf_op jit(solution)/shard_map/ppermute | solution.py:14
  54.3 24.6 %collective-permute-start.4 = (f32[4,128,128]{2,1,0:T(8,128)}, f32[4,128,128]{2,1,0:T(8,128)}, u32[]{:S(2)}, u32[]{:S(2)}) collective-permute-start(f32[4,128,128]{2,1,0:T(8,128)} %get-tuple-element.31), channel_id=1, source_target_pairs={{0,1},{1,0},{2,3},{3,2},{4,5},{5,4},{6,7},{7,6},{8,9},{9,8},{10,11... | collective-permute-start | bytes 786440 | tf_op jit(solution)/shard_map/ppermute | solution.py:14
  55.0 11.6 %copy-start.8 = (f32[1,4,128,128]{3,2,1,0:T(8,128)S(1)}, f32[1,4,128,128]{3,2,1,0:T(8,128)}, u32[]{:S(2)}) copy-start(f32[1,4,128,128]{3,2,1,0:T(8,128)} %copy-done.7) | copy-start | bytes 786436
  55.0 11.6 %copy-start.10 = (f32[1,4,128,128]{3,2,1,0:T(8,128)S(1)}, f32[1,4,128,128]{3,2,1,0:T(8,128)}, u32[]{:S(2)}) copy-start(f32[1,4,128,128]{3,2,1,0:T(8,128)} %copy-done.9) | copy-start | bytes 786436
  55.0 11.6 %copy-start.12 = (f32[1,4,128,128]{3,2,1,0:T(8,128)S(1)}, f32[1,4,128,128]{3,2,1,0:T(8,128)}, u32[]{:S(2)}) copy-start(f32[1,4,128,128]{3,2,1,0:T(8,128)} %get-tuple-element.41) | copy-start | bytes 786436
  55.0 11.6 %copy-start.14 = (f32[1,4,128,128]{3,2,1,0:T(8,128)S(1)}, f32[1,4,128,128]{3,2,1,0:T(8,128)}, u32[]{:S(2)}) copy-start(f32[1,4,128,128]{3,2,1,0:T(8,128)} %copy-done.13) | copy-start | bytes 786436
  56.9 9.2 %collective-permute-start.11 = (f32[4,128,128]{2,1,0:T(8,128)S(1)}, f32[4,128,128]{2,1,0:T(8,128)S(1)}, u32[]{:S(2)}, u32[]{:S(2)}) collective-permute-start(f32[4,128,128]{2,1,0:T(8,128)S(1)} %get-tuple-element.36), channel_id=1, source_target_pairs={{0,2},{1,3},{2,0},{3,1},{4,6},{5,7},{6,4},{7,5},{8,10},{9,11},{10,... | collective-permute-start | bytes 786440 | tf_op jit(solution)/shard_map/ppermute | solution.py:14
  58.1 10.3 %copy-start.42 = (f32[4,13,256]{2,0,1:T(4,128)}, f32[4,13,256]{2,0,1:T(4,128)S(1)}, u32[]{:S(2)}) copy-start(f32[4,13,256]{2,0,1:T(4,128)S(1)} %constant_dynamic-update-slice_fusion) | copy-start | bytes 159748
  58.4 14.0 %collective-permute-start.8 = (f32[4,128,128]{2,1,0:T(8,128)S(1)}, f32[4,128,128]{2,1,0:T(8,128)}, u32[]{:S(2)}, u32[]{:S(2)}) collective-permute-start(f32[4,128,128]{2,1,0:T(8,128)S(1)} %get-tuple-element.37), channel_id=1, source_target_pairs={{0,2},{1,3},{2,0},{3,1},{4,6},{5,7},{6,4},{7,5},{8,10},{9,11},{10,... | collective-permute-start | bytes 786440 | tf_op jit(solution)/shard_map/ppermute | solution.py:14
  66.1 8.6 %collective-permute-start.12 = (f32[4,128,128]{2,1,0:T(8,128)S(1)}, f32[4,128,128]{2,1,0:T(8,128)}, u32[]{:S(2)}, u32[]{:S(2)}) collective-permute-start(f32[4,128,128]{2,1,0:T(8,128)S(1)} %add.371), channel_id=1, source_target_pairs={{0,4},{1,5},{2,6},{3,7},{4,0},{5,1},{6,2},{7,3},{8,12},{9,13},{10,... | collective-permute-start | bytes 786440 | tf_op jit(solution)/shard_map/ppermute | solution.py:14
  68.4 2.4 %copy-start.15 = (f32[4,128,128]{2,1,0:T(8,128)S(1)}, f32[4,128,128]{2,1,0:T(8,128)}, u32[]{:S(2)}) copy-start(f32[4,128,128]{2,1,0:T(8,128)} %get-tuple-element.35) | copy-start | bytes 786436
  70.8 8.1 %collective-permute-start.6 = (f32[4,128,128]{2,1,0:T(8,128)S(1)}, f32[4,128,128]{2,1,0:T(8,128)S(1)}, u32[]{:S(2)}, u32[]{:S(2)}) collective-permute-start(f32[4,128,128]{2,1,0:T(8,128)S(1)} %copy-done.15), channel_id=1, source_target_pairs={{0,2},{1,3},{2,0},{3,1},{4,6},{5,7},{6,4},{7,5},{8,10},{9,11},{10,... | collective-permute-start | bytes 786440 | tf_op jit(solution)/shard_map/ppermute | solution.py:14
  73.4 11.4 %collective-permute-start.9 = (f32[4,128,128]{2,1,0:T(8,128)S(1)}, f32[4,128,128]{2,1,0:T(8,128)S(1)}, u32[]{:S(2)}, u32[]{:S(2)}) collective-permute-start(f32[4,128,128]{2,1,0:T(8,128)S(1)} %add.368), channel_id=1, source_target_pairs={{0,4},{1,5},{2,6},{3,7},{4,0},{5,1},{6,2},{7,3},{8,12},{9,13},{10,... | collective-permute-start | bytes 786440 | tf_op jit(solution)/shard_map/ppermute | solution.py:14
  75.8 12.4 %collective-permute-start.13 = (f32[4,128,128]{2,1,0:T(8,128)S(1)}, f32[4,128,128]{2,1,0:T(8,128)S(1)}, u32[]{:S(2)}, u32[]{:S(2)}) collective-permute-start(f32[4,128,128]{2,1,0:T(8,128)S(1)} %add.372), channel_id=1, source_target_pairs={{0,8},{1,9},{2,10},{3,11},{4,12},{5,13},{6,14},{7,15},{8,0},{9,1},... | collective-permute-start | bytes 786440 | tf_op jit(solution)/shard_map/ppermute | solution.py:14
  (9 other events, 17.5 us)
